TPU v7x, 512 devices: a whole 4x8x8 slice. The times are simulated.
512 devices in a mesh: dp: 16 (over z, core), ctx: 32 (over y, x).
Axes of the slice: x: 4, y: 8, z: 8, core: 2. Of those that a mesh axis runs over, the one named last changes fastest.
Arguments:
- query_in: bfloat16 [16, 8192, 1280], P('dp', 'ctx'), may hold values from -150 to 150
- key_in: bfloat16 [16, 8192, 1280], P('dp', 'ctx'), may hold values from -16 to 16
- value_in: bfloat16 [16, 8192, 1280], P('dp', 'ctx'), may hold values from -6 to 6
- grad_out: bfloat16 [16, 8192, 1280], P('dp', 'ctx'), may hold values from -6 to 6
- key_blocks: int32 [10, 32, 6], P(None, 'ctx'), may hold values from 0 to 63, as said below
- sink_logits: float32 [10], replicated, may hold values from 3 to 8
Outputs:
- grad_query: bfloat16 [16, 8192, 1280], P('dp', 'ctx')
- grad_key: bfloat16 [16, 8192, 1280], P('dp', 'ctx')
- grad_value: bfloat16 [16, 8192, 1280], P('dp', 'ctx')
- grad_sink: float32 [10], replicated
Inputs may be any that keep to these rules, and one draw needn't show every extreme that they name: `key_blocks`: block b holds tokens 128 b to 128 b + 127. The 6 entries of one head and segment are distinct, and none falls in the aligned group of 256 tokens that holds the segment. Counting all heads, entries and segments of one aligned group of 256 tokens, at most 2 entries fall in any one other aligned group of 256 tokens, and every group reaches 2 with some other group in every draw.
All inputs are finite; a program needn't handle non-finite values.
Results may differ from a plain program's by a relative error of at most 0.012.
Values may be sent and summed in bfloat16 or wider, within the bound.
A program may use at most 64 MiB of HBM per device.

v0:
```python
from functools import partial
import math
import jax
import jax.numpy as jnp
from jax import lax
from jax.sharding import PartitionSpec as P

BLOCK = 128


def slot_layout(block_rows, groups, per_group, capacity):
    head_count, segments, listed = block_rows.shape
    ordered = jnp.transpose(block_rows, (2, 0, 1)).reshape(-1)
    head_ids = jnp.broadcast_to(
        jnp.arange(head_count, dtype=jnp.int32)[None, :, None], (listed, head_count, segments)
    ).reshape(-1)
    owners = ordered // per_group
    req_codes = head_ids * per_group + ordered % per_group
    positions = jnp.arange(ordered.shape[0], dtype=jnp.int32)
    earlier = (owners[:, None] == owners[None, :]) & (positions[None, :] < positions[:, None])
    places = owners * capacity + jnp.sum(earlier.astype(jnp.int32), axis=1)
    targets = jnp.arange(groups * capacity, dtype=jnp.int32)
    matched = places[None, :] == targets[:, None]
    filled = jnp.any(matched, axis=1)
    source_ids = jnp.sum(jnp.where(matched, positions[None, :], 0), axis=1)
    sent_codes = jnp.where(filled, jnp.sum(jnp.where(matched, req_codes[None, :], 0), axis=1), -1)
    return (places, filled, source_ids, sent_codes.reshape(groups, capacity))


def log_total(scores, sink_grp):
    sink_side = sink_grp[:, None, None]
    row_top = jnp.maximum(jnp.max(scores, axis=-1), sink_side)
    row_total = jnp.exp(sink_side - row_top) + jnp.sum(
        jnp.exp(scores - row_top[..., None]), axis=-1
    )
    return row_top + jnp.log(row_total)


def forward_group(inputs, scaling):
    query_grp, local_kv, remote_kv, sink_grp = inputs
    head_dim = query_grp.shape[-1]
    kv_all = jnp.concatenate([local_kv, remote_kv], axis=2)
    scores = (
        jnp.einsum(
            "gsqd,gskd->gsqk", query_grp, kv_all[..., :head_dim], preferred_element_type=jnp.float32
        )
        * scaling
    )
    log_norm = log_total(scores, sink_grp)
    prob_bf = jnp.exp(scores - log_norm[..., None]).astype(jnp.bfloat16)
    attended = jnp.einsum(
        "gsqk,gskd->gsqd", prob_bf, kv_all[..., head_dim:], preferred_element_type=jnp.float32
    )
    return (attended.astype(jnp.bfloat16), log_norm)


def backward_group(inputs, scaling, seg_len):
    query_grp, local_kv, remote_kv, sink_grp, grad_grp, attended, log_norm = inputs
    head_dim = query_grp.shape[-1]
    kv_all = jnp.concatenate([local_kv, remote_kv], axis=2)
    scores = (
        jnp.einsum(
            "gsqd,gskd->gsqk", query_grp, kv_all[..., :head_dim], preferred_element_type=jnp.float32
        )
        * scaling
    )
    weights = jnp.exp(scores - log_norm[..., None])
    prob_bf = weights.astype(jnp.bfloat16)
    row_delta = jnp.sum(grad_grp.astype(jnp.float32) * attended.astype(jnp.float32), axis=-1)
    dprobs = jnp.einsum(
        "gsqd,gskd->gsqk", grad_grp, kv_all[..., head_dim:], preferred_element_type=jnp.float32
    )
    dscores = (weights * (dprobs - row_delta[..., None])).astype(jnp.bfloat16)
    grad_q = (
        jnp.einsum(
            "gsqk,gskd->gsqd", dscores, kv_all[..., :head_dim], preferred_element_type=jnp.float32
        )
        * scaling
    )
    key_terms = (
        jnp.einsum("gsqk,gsqd->gskd", dscores, query_grp, preferred_element_type=jnp.float32)
        * scaling
    )
    value_terms = jnp.einsum(
        "gsqk,gsqd->gskd", prob_bf, grad_grp, preferred_element_type=jnp.float32
    )
    all_terms = jnp.concatenate([key_terms, value_terms], axis=-1)
    sink_part = -jnp.sum(jnp.exp(sink_grp[:, None, None] - log_norm) * row_delta, axis=(1, 2))
    return (
        grad_q.astype(jnp.bfloat16),
        all_terms[:, :, :seg_len],
        all_terms[:, :, seg_len:].astype(jnp.bfloat16),
        sink_part,
    )


def body(query_in, key_in, value_in, grad_out, key_blocks, sink_logits):
    groups = lax.axis_size("ctx")
    head_count = sink_logits.shape[0]
    tok_dev = query_in.shape[1]
    head_dim = query_in.shape[2] // head_count
    seg_per_dev = key_blocks.shape[1]
    listed = key_blocks.shape[2]
    seg_len = tok_dev // seg_per_dev
    per_group = tok_dev // BLOCK
    requests = head_count * seg_per_dev * listed
    capacity = (requests + groups - 2) // (groups - 1)
    scaling = 1.0 / math.sqrt(head_dim)
    pair_heads = 2
    pair_count = head_count // pair_heads
    double_dim = 2 * head_dim
    places, filled, source_ids, sent_codes = slot_layout(key_blocks, groups, per_group, capacity)
    recv_codes = lax.all_to_all(sent_codes, "ctx", split_axis=0, concat_axis=0, tiled=True)
    local_kv = jnp.concatenate(
        [
            key_in[0].reshape(per_group, BLOCK, head_count, head_dim),
            value_in[0].reshape(per_group, BLOCK, head_count, head_dim),
        ],
        axis=-1,
    )
    safe_codes = jnp.maximum(recv_codes, 0)
    payload = local_kv[safe_codes % per_group, :, safe_codes // per_group, :]

    def arrange_remote(fetched):
        flat_slots = fetched.reshape(groups * capacity, BLOCK, double_dim)
        remote_rows = flat_slots[places].reshape(listed, head_count, seg_per_dev, BLOCK, double_dim)
        remote_rows = jnp.transpose(remote_rows, (1, 2, 0, 3, 4))
        return remote_rows.reshape(pair_count, pair_heads, seg_per_dev, listed * BLOCK, double_dim)

    def to_pairs(field):
        columns = field.shape[-1]
        split = jnp.transpose(
            field.reshape(seg_per_dev, seg_len, head_count, columns), (2, 0, 1, 3)
        )
        return split.reshape(pair_count, pair_heads, seg_per_dev, seg_len, columns)

    fetched = lax.all_to_all(payload, "ctx", split_axis=0, concat_axis=0, tiled=True)
    remote_pairs = arrange_remote(fetched)
    query_pairs = to_pairs(query_in[0].reshape(tok_dev, head_count, head_dim))
    grad_pairs = to_pairs(grad_out[0].reshape(tok_dev, head_count, head_dim))
    local_pairs = to_pairs(local_kv.reshape(tok_dev, head_count, double_dim))
    sink_pairs = sink_logits.reshape(pair_count, pair_heads)
    attended, log_norm = lax.map(
        partial(forward_group, scaling=scaling),
        (query_pairs, local_pairs, remote_pairs, sink_pairs),
    )
    back_remote = arrange_remote(
        lax.all_to_all(payload, "ctx", split_axis=0, concat_axis=0, tiled=True)
    )
    grad_q, own_terms, list_terms, sink_parts = lax.map(
        partial(backward_group, scaling=scaling, seg_len=seg_len),
        (query_pairs, local_pairs, back_remote, sink_pairs, grad_pairs, attended, log_norm),
    )
    grad_query = jnp.transpose(
        grad_q.reshape(head_count, seg_per_dev, seg_len, head_dim), (1, 2, 0, 3)
    )
    grad_query = grad_query.reshape(1, tok_dev, head_count * head_dim)
    own_flat = jnp.transpose(
        own_terms.reshape(head_count, seg_per_dev, seg_len, double_dim), (1, 2, 0, 3)
    )
    own_flat = own_flat.reshape(tok_dev, head_count, double_dim)
    list_rows = jnp.transpose(
        list_terms.reshape(head_count, seg_per_dev, listed, BLOCK, double_dim), (2, 0, 1, 3, 4)
    )
    list_rows = list_rows.reshape(requests, BLOCK, double_dim)
    send_back = jnp.where(filled[:, None, None], list_rows[source_ids], jnp.zeros((), jnp.bfloat16))
    returned = lax.all_to_all(
        send_back.reshape(groups, capacity, BLOCK, double_dim),
        "ctx",
        split_axis=0,
        concat_axis=0,
        tiled=True,
    )
    selector = (
        recv_codes.reshape(-1)[:, None]
        == jnp.arange(head_count * per_group, dtype=jnp.int32)[None, :]
    ).astype(jnp.bfloat16)
    incoming = jnp.einsum(
        "pj,pbe->jbe",
        selector,
        returned.reshape(groups * capacity, BLOCK, double_dim),
        preferred_element_type=jnp.float32,
    )
    incoming = jnp.transpose(
        incoming.reshape(head_count, per_group, BLOCK, double_dim), (1, 2, 0, 3)
    )
    combined = own_flat + incoming.reshape(tok_dev, head_count, double_dim)
    grad_key = (
        combined[..., :head_dim].astype(jnp.bfloat16).reshape(1, tok_dev, head_count * head_dim)
    )
    grad_value = (
        combined[..., head_dim:].astype(jnp.bfloat16).reshape(1, tok_dev, head_count * head_dim)
    )
    grad_sink = lax.psum(sink_parts.reshape(head_count), ("dp", "ctx"))
    return (grad_query, grad_key, grad_value, grad_sink)


def solution(mesh):
    placed = (
        P("dp", "ctx", None),
        P("dp", "ctx", None),
        P("dp", "ctx", None),
        P("dp", "ctx", None),
        P(None, "ctx", None),
        P(),
    )
    return jax.shard_map(
        body,
        mesh=mesh,
        in_specs=placed,
        out_specs=(P("dp", "ctx", None), P("dp", "ctx", None), P("dp", "ctx", None), P()),
        check_vma=False,
    )
```

profile of v0, /device:TPU:27, one launch (start us, length us, event | category | flops | bytes accessed | tf_op | source)
XLA Modules:
  0.0 474.1 jit_solution(14421471684461468160)
XLA Ops:
  2.7 9.4 %all-to-all-start = ((s32[32,1,2]{2,1,0:T(1,128)}), s32[32,1,2]{2,1,0:T(1,128)S(1)}, u32[]{:S(2)}, u32[]{:S(2)}) async-start(s32[32,1,2]{2,1,0:T(1,128)} %bitcast.31), calls=%async_computation | async-start | bytes 32768 | tf_op jit(solution)/shard_map/all_to_all | solution.py:113
  12.0 1.5 reshape.729
  14.4 2.6 all-to-all-done
  17.3 2.8 gather_fusion
  20.1 8.4 %all-to-all-start.1 = ((bf16[32,2,128,256]{3,2,1,0:T(8,128)(2,1)}), bf16[32,2,128,256]{3,2,1,0:T(8,128)(2,1)}, u32[]{:S(2)}, u32[]{:S(2)}) async-start(bf16[32,2,128,256]{3,2,1,0:T(8,128)(2,1)} %bitcast.232), calls=%async_computation.1 | async-start | bytes 8388608 | tf_op jit(solution)/shard_map/all_to_all | solution.py:148
  29.9 1.1 copy.160
  30.9 2.2 copy.159
  33.2 1.5 copy.161
  34.7 83.7 %all-to-all-done.1 = bf16[32,2,128,256]{3,2,1,0:T(8,128)(2,1)} async-done(((bf16[32,2,128,256]{3,2,1,0:T(8,128)(2,1)}), bf16[32,2,128,256]{3,2,1,0:T(8,128)(2,1)}, u32[]{:S(2)}, u32[]{:S(2)}) %all-to-all-start.1) | async-done | bytes 4194336 | tf_op jit(solution)/shard_map/all_to_all | solution.py:148
  118.4 4.9 %gather_fusion.1 = bf16[60,128,256]{2,1,0:T(8,128)(2,1)} fusion(bf16[64,128,256]{2,1,0:T(8,128)(2,1)} %bitcast.36, s32[1024]{0:T(1024)S(1)} %pad_clamp_fusion.1), kind=kCustom, calls=%fused_computation.1 | custom fusion | bytes 7864560 | tf_op jit(solution)/shard_map/gather | solution.py:126
  123.2 4.4 copy.155
  127.7 28.0 %while.28 = (s32[]{:T(128)}, bf16[5,2,1,256,128]{4,3,1,2,0:T(8,128)(2,1)}, f32[5,2,1,256]{3,1,2,0:T(2,128)S(1)}, bf16[5,2,1,256,128]{4,3,1,2,0:T(8,128)(2,1)}, b...) while((s32[]{:T(128)}, ...), condition=%wide.region_6.7_spmd, body=%wide.region_3.6_spmd.sunk | while | flops 274796032 | bytes 10773141 | solution.py:143
  128.7 1.2 dynamic-slice_bitcast_fusion.9
  129.9 1.4 multiply_reduce_fusion.6
  131.9 1.2 fusion.95
  134.3 1.2 dynamic-slice_bitcast_fusion.9
  135.5 1.4 multiply_reduce_fusion.6
  137.6 1.2 fusion.95
  139.9 1.2 dynamic-slice_bitcast_fusion.9
  141.1 1.4 multiply_reduce_fusion.6
  143.2 1.2 fusion.95
  145.5 1.2 dynamic-slice_bitcast_fusion.9
  146.7 1.4 multiply_reduce_fusion.6
  148.8 1.2 fusion.95
  151.1 1.2 dynamic-slice_bitcast_fusion.9
  152.3 1.4 multiply_reduce_fusion.6
  154.4 1.2 fusion.95
  155.7 69.4 %while.29 = (s32[]{:T(128)}, bf16[5,2,1,256,128]{3,4,1,0,2:T(8,128)(2,1)}, f32[5,2,1,256,256]{3,4,1,2,0:T(8,128)}, bf16[5,2,1,768,256]{4,3,1,0,2:T(8,128)(2,1)},...) while((s32[]{:T(128)}, ...), condition=%wide.region_10.11_spmd, body=%wide.region_7.10_spmd.sunk | while | flops 680788992 | bytes 27408636 | solution.py:150
  156.8 1.1 multiply_reduce_fusion.7
  159.1 1.2 dynamic-slice_bitcast_fusion.11
  160.3 1.3 fusion.107
  163.4 1.3 fusion.110
  166.4 1.4 copy.191
  170.7 1.1 multiply_reduce_fusion.7
  173.0 1.2 dynamic-slice_bitcast_fusion.11
  174.2 1.3 fusion.107
  177.3 1.3 fusion.110
  180.3 1.4 copy.191
  186.9 1.2 dynamic-slice_bitcast_fusion.11
  188.1 1.3 fusion.107
  191.2 1.3 fusion.110
  194.2 1.4 copy.191
  198.5 1.1 multiply_reduce_fusion.7
  200.8 1.2 dynamic-slice_bitcast_fusion.11
  201.9 1.3 fusion.107
  205.1 1.3 fusion.110
  208.1 1.4 copy.191
  214.6 1.2 dynamic-slice_bitcast_fusion.11
  215.8 1.3 fusion.107
  218.9 1.3 fusion.110
  222.0 1.4 copy.191
  225.2 4.4 copy.166
  229.6 4.9 %gather_fusion.2 = bf16[64,128,256]{2,1,0:T(8,128)(2,1)} fusion(bf16[60,128,256]{2,1,0:T(8,128)(2,1)} %bitcast.231, s32[1024]{0:T(1024)S(1)} %pad_clamp_fusion), kind=kCustom, calls=%fused_computation.2 | custom fusion | bytes 8388864 | tf_op jit(solution)/shard_map/gather | solution.py:166
  234.4 9.1 %broadcast_select_fusion = bf16[32,2,128,256]{3,1,2,0:T(2,128)(2,1)} fusion(pred[32,2]{1,0:T(8,128)(4,1)S(1)} %broadcast_in_dim.98, bf16[32,2,128,256]{3,2,1,0:T(8,128)(2,1)} %bitcast.234), kind=kLoop, calls=%fused_computation.85 | loop fusion | flops 2097152 | bytes 8388672 | tf_op jit(solution)/shard_map/jit(_where)/select_n | solution.py:166
  243.5 9.7 %all-to-all-start.2 = ((bf16[32,2,128,256]{3,1,2,0:T(2,128)(2,1)}), bf16[32,2,128,256]{3,1,2,0:T(2,128)(2,1)}, u32[]{:S(2)}, u32[]{:S(2)}) async-start(bf16[32,2,128,256]{3,1,2,0:T(2,128)(2,1)} %broadcast_select_fusion), calls=%async_computation.2 | async-start | bytes 8388608 | tf_op jit(solution)/shard_map/all_to_all | solution.py:167
  254.7 188.4 %psum.7 = f32[10]{0:T(128)} all-reduce(f32[10]{0:T(128)S(1)} %reshape.704), channel_id=1, replica_groups=mesh['dp'=16,'ctx'=32] {'dp','ctx'}, use_global_device_ids=true, to_apply=%region_12.13 | all-reduce | flops 10 | bytes 80 | tf_op jit(solution)/shard_map/psum | solution.py:194
  443.0 2.2 copy.170
  445.2 8.9 %copy.168 = bf16[32,2,128,256]{3,1,0,2:T(2,128)(2,1)} copy(bf16[32,2,128,256]{3,1,2,0:T(2,128)(2,1)} %all-to-all-done.2) | data formatting | bytes 8388608 | tf_op jit(solution)/shard_map/all_to_all | solution.py:167
  454.1 7.2 %reshape.728 = bf16[64,128,256,1]{2,0,1,3:T(8,128)(2,1)} reshape(bf16[32,2,128,256]{3,1,0,2:T(2,128)(2,1)} %copy.168) | data formatting | bytes 8388608 | tf_op jit(solution)/shard_map/reshape | solution.py:181
  461.3 4.9 %fusion.56 = f32[10,2,128,256]{3,0,2,1:T(8,128)} fusion(bf16[64,128,256,1]{2,0,1,3:T(8,128)(2,1)} %reshape.728, s32[10,2]{0,1:T(2,128)S(1)} %multiply_add_fusion, s32[64]{0:T(128)S(1)} %eq.67), kind=kOutput, calls=%fused_computation.97 | convolution fusion | flops 83887360 | bytes 6816080 | tf_op jit(solution)/shard_map/pj,pbe->jbe/dot_general | solution.py:178
  466.2 3.4 copy.169
  469.6 2.2 fusion.53
  471.9 1.1 copy.172
  473.0 1.1 copy.171
  (162 shorter events, 54.6 us)
Async XLA Ops:
  0.6 0.7 copy-start
  0.6 13.0 %copy-start.3 = (bf16[1,256,1280]{2,1,0:T(8,128)(2,1)S(1)}, bf16[1,256,1280]{2,1,0:T(8,128)(2,1)}, u32[]{:S(2)}) copy-start(bf16[1,256,1280]{2,1,0:T(8,128)(2,1)} %param.12) | copy-start | bytes 1966084
  2.7 14.4 %all-to-all-start = ((s32[32,1,2]{2,1,0:T(1,128)}), s32[32,1,2]{2,1,0:T(1,128)S(1)}, u32[]{:S(2)}, u32[]{:S(2)}) async-start(s32[32,1,2]{2,1,0:T(1,128)} %bitcast.31), calls=%async_computation | async-start | bytes 32768 | tf_op jit(solution)/shard_map/all_to_all | solution.py:113
  20.1 8.6 %copy-start.2 = (bf16[1,256,1280]{2,1,0:T(8,128)(2,1)S(1)}, bf16[1,256,1280]{2,1,0:T(8,128)(2,1)}, u32[]{:S(2)}) copy-start(bf16[1,256,1280]{2,1,0:T(8,128)(2,1)} %param.11) | copy-start | bytes 1966084
  20.1 98.2 %all-to-all-start.1 = ((bf16[32,2,128,256]{3,2,1,0:T(8,128)(2,1)}), bf16[32,2,128,256]{3,2,1,0:T(8,128)(2,1)}, u32[]{:S(2)}, u32[]{:S(2)}) async-start(bf16[32,2,128,256]{3,2,1,0:T(8,128)(2,1)} %bitcast.232), calls=%async_computation.1 | async-start | bytes 8388608 | tf_op jit(solution)/shard_map/all_to_all | solution.py:148
  28.5 0.8 copy-start.5
  28.5 1.1 copy-start.4
  243.5 201.7 %all-to-all-start.2 = ((bf16[32,2,128,256]{3,1,2,0:T(2,128)(2,1)}), bf16[32,2,128,256]{3,1,2,0:T(2,128)(2,1)}, u32[]{:S(2)}, u32[]{:S(2)}) async-start(bf16[32,2,128,256]{3,1,2,0:T(2,128)(2,1)} %broadcast_select_fusion), calls=%async_computation.2 | async-start | bytes 8388608 | tf_op jit(solution)/shard_map/all_to_all | solution.py:167
  469.6 4.5 copy-start.1
where the time goes:
time: 476 us; the launch traced here: 474 us
  blocking collectives  188 us (39%)
  local copies, waits for them, and re-layouts  98.7 us (21%)
  waiting for transfers between devices  86.3 us (18%)
  matrix products  40.1 us (8%)
  other arithmetic  31.8 us (7%)
  starting transfers between devices  27.5 us (6%)
    psum x1, blocking collectives, body(): grad_sink = lax.psum(sink_parts.reshape(head_count), ('dp', 'ctx'))  188 us
    all_to_all x1, waiting for transfers between devices, body(): lax.all_to_all(payload, 'ctx', split_axis=0, concat_axis=0, tiled=True)  83.7 us
    squeeze x20, local copies, waits for them, and re-layouts, body(): lax.map(partial(forward_group, scaling=scaling), (query_pairs, local_pair...  21.6 us
    dynamic_update_slice x15, local copies, waits for them, and re-layouts, body(): lax.map(partial(backward_group, scaling=scaling, seg_len=seg_len), (query...  11.9 us
    all_to_all x1, starting transfers between devices, body(): lax.all_to_all(send_back.reshape(groups, capacity, BLOCK, double_dim), 'c...  9.72 us
  transfers between devices with their start and end apart: 3, of which 2 were waited for; matrix products, arithmetic and copies ran while one was open for 2% of the time, Pallas kernels for 0%

commit v1 on v0

--- a/solution.py
+++ b/solution.py
@@ -191,7 +191,7 @@
     grad_value = (
         combined[..., head_dim:].astype(jnp.bfloat16).reshape(1, tok_dev, head_count * head_dim)
     )
-    grad_sink = lax.psum(sink_parts.reshape(head_count), ("dp", "ctx"))
+    grad_sink = lax.psum(lax.psum(sink_parts.reshape(head_count), "dp"), "ctx")
     return (grad_query, grad_key, grad_value, grad_sink)
 
 

time: 476 us -> 442 us (0.929)
  the two profiles are of different devices: /device:TPU:27 before, /device:TPU:354 now
where the time goes in v1:
time: 442 us; the launch traced here: 440 us
  blocking collectives  152 us (34%)
  local copies, waits for them, and re-layouts  98.7 us (22%)
  waiting for transfers between devices  85.6 us (19%)
  matrix products  40.1 us (9%)
  other arithmetic  31.8 us (7%)
  starting transfers between devices  30.5 us (7%)
    psum x2, blocking collectives, body(): grad_sink = lax.psum(lax.psum(sink_parts.reshape(head_count), 'dp'), 'ctx')  152 us
    all_to_all x1, waiting for transfers between devices, body(): lax.all_to_all(payload, 'ctx', split_axis=0, concat_axis=0, tiled=True)  84.3 us
    squeeze x20, local copies, waits for them, and re-layouts, body(): lax.map(partial(forward_group, scaling=scaling), (query_pairs, local_pair...  21.6 us
    dynamic_update_slice x15, local copies, waits for them, and re-layouts, body(): lax.map(partial(backward_group, scaling=scaling, seg_len=seg_len), (query...  11.9 us
    all_to_all x1, starting transfers between devices, body(): lax.all_to_all(payload, 'ctx', split_axis=0, concat_axis=0, tiled=True)  10.8 us
    all_to_all x1, starting transfers between devices, body(): lax.all_to_all(send_back.reshape(groups, capacity, BLOCK, double_dim), 'c...  9.92 us
    all_to_all x1, starting transfers between devices, body(): lax.all_to_all(sent_codes, 'ctx', split_axis=0, concat_axis=0, tiled=True)  9.8 us
    select_n x1, other arithmetic, body(): jnp.where(filled[:, None, None], list_rows[source_ids], jnp.zeros((), jnp...  9.07 us
  transfers between devices with their start and end apart: 3, of which 2 were waited for; matrix products, arithmetic and copies ran while one was open for 3% of the time, Pallas kernels for 0%

profile of v1, /device:TPU:354, one launch (start us, length us, event | category | flops | bytes accessed | tf_op | source)
XLA Modules:
  0.0 440.0 jit_solution(5020441362807392879)
XLA Ops:
  2.7 9.8 %all-to-all-start = ((s32[32,1,2]{2,1,0:T(1,128)}), s32[32,1,2]{2,1,0:T(1,128)S(1)}, u32[]{:S(2)}, u32[]{:S(2)}) async-start(s32[32,1,2]{2,1,0:T(1,128)} %bitcast.31), calls=%async_computation | async-start | bytes 32768 | tf_op jit(solution)/shard_map/all_to_all | solution.py:113
  12.5 1.5 reshape.729
  14.9 1.4 all-to-all-done
  16.6 2.8 gather_fusion
  19.4 10.8 %all-to-all-start.1 = ((bf16[32,2,128,256]{3,2,1,0:T(8,128)(2,1)}), bf16[32,2,128,256]{3,2,1,0:T(8,128)(2,1)}, u32[]{:S(2)}, u32[]{:S(2)}) async-start(bf16[32,2,128,256]{3,2,1,0:T(8,128)(2,1)} %bitcast.232), calls=%async_computation.1 | async-start | bytes 8388608 | tf_op jit(solution)/shard_map/all_to_all | solution.py:148
  31.5 1.1 copy.160
  32.6 2.2 copy.159
  34.8 1.5 copy.161
  36.3 84.3 %all-to-all-done.1 = bf16[32,2,128,256]{3,2,1,0:T(8,128)(2,1)} async-done(((bf16[32,2,128,256]{3,2,1,0:T(8,128)(2,1)}), bf16[32,2,128,256]{3,2,1,0:T(8,128)(2,1)}, u32[]{:S(2)}, u32[]{:S(2)}) %all-to-all-start.1) | async-done | bytes 4194336 | tf_op jit(solution)/shard_map/all_to_all | solution.py:148
  120.6 4.9 %gather_fusion.1 = bf16[60,128,256]{2,1,0:T(8,128)(2,1)} fusion(bf16[64,128,256]{2,1,0:T(8,128)(2,1)} %bitcast.36, s32[1024]{0:T(1024)S(1)} %pad_clamp_fusion.1), kind=kCustom, calls=%fused_computation.1 | custom fusion | bytes 7864560 | tf_op jit(solution)/shard_map/gather | solution.py:126
  125.5 4.4 %copy.155 = bf16[10,1,6,128,256]{4,3,2,0,1:T(8,128)(2,1)} copy(bf16[10,1,6,128,256]{4,3,0,2,1:T(8,128)(2,1)} %bitcast.235) | data formatting | bytes 7864320 | tf_op jit(solution)/shard_map/transpose | solution.py:127
  129.9 28.0 %while.28 = (s32[]{:T(128)}, bf16[5,2,1,256,128]{4,3,1,2,0:T(8,128)(2,1)}, f32[5,2,1,256]{3,1,2,0:T(2,128)S(1)}, bf16[5,2,1,256,128]{4,3,1,2,0:T(8,128)(2,1)}, b...) while((s32[]{:T(128)}, ...), condition=%wide.region_6.7_spmd, body=%wide.region_3.6_spmd.sunk | while | flops 274796032 | bytes 10773141 | solution.py:143
  130.9 1.2 dynamic-slice_bitcast_fusion.9
  132.1 1.4 multiply_reduce_fusion.6
  134.2 1.2 fusion.95
  136.5 1.2 dynamic-slice_bitcast_fusion.9
  137.7 1.4 multiply_reduce_fusion.6
  139.8 1.2 fusion.95
  142.1 1.2 dynamic-slice_bitcast_fusion.9
  143.3 1.4 multiply_reduce_fusion.6
  145.4 1.2 fusion.95
  147.7 1.2 dynamic-slice_bitcast_fusion.9
  148.9 1.4 multiply_reduce_fusion.6
  151.0 1.2 fusion.95
  153.3 1.2 dynamic-slice_bitcast_fusion.9
  154.5 1.4 multiply_reduce_fusion.6
  156.6 1.2 fusion.95
  157.9 69.4 %while.29 = (s32[]{:T(128)}, bf16[5,2,1,256,128]{3,4,1,0,2:T(8,128)(2,1)}, f32[5,2,1,256,256]{3,4,1,2,0:T(8,128)}, bf16[5,2,1,768,256]{4,3,1,0,2:T(8,128)(2,1)},...) while((s32[]{:T(128)}, ...), condition=%wide.region_10.11_spmd, body=%wide.region_7.10_spmd.sunk | while | flops 680788992 | bytes 27408636 | solution.py:150
  159.0 1.1 multiply_reduce_fusion.7
  161.3 1.2 dynamic-slice_bitcast_fusion.11
  162.5 1.3 fusion.107
  165.6 1.3 fusion.110
  168.6 1.4 copy.191
  172.9 1.1 multiply_reduce_fusion.7
  175.2 1.2 dynamic-slice_bitcast_fusion.11
  176.4 1.3 fusion.107
  179.5 1.3 fusion.110
  182.5 1.4 copy.191
  189.1 1.2 dynamic-slice_bitcast_fusion.11
  190.3 1.3 fusion.107
  193.4 1.3 fusion.110
  196.4 1.4 copy.191
  202.9 1.2 dynamic-slice_bitcast_fusion.11
  204.1 1.3 fusion.107
  207.3 1.3 fusion.110
  210.3 1.4 copy.191
  216.8 1.2 dynamic-slice_bitcast_fusion.11
  218.0 1.3 fusion.107
  221.1 1.3 fusion.110
  224.2 1.4 copy.191
  227.4 4.4 %copy.166 = bf16[6,10,1,128,256]{4,3,1,0,2:T(8,128)(2,1)} copy(bf16[6,10,1,128,256]{4,3,0,1,2:T(8,128)(2,1)} %bitcast.237) | data formatting | bytes 7864320 | tf_op jit(solution)/shard_map/transpose | solution.py:162
  231.8 4.9 %gather_fusion.2 = bf16[64,128,256]{2,1,0:T(8,128)(2,1)} fusion(bf16[60,128,256]{2,1,0:T(8,128)(2,1)} %bitcast.231, s32[1024]{0:T(1024)S(1)} %pad_clamp_fusion), kind=kCustom, calls=%fused_computation.2 | custom fusion | bytes 8388864 | tf_op jit(solution)/shard_map/gather | solution.py:166
  236.6 9.1 %broadcast_select_fusion = bf16[32,2,128,256]{3,1,2,0:T(2,128)(2,1)} fusion(pred[32,2]{1,0:T(8,128)(4,1)S(1)} %broadcast_in_dim.98, bf16[32,2,128,256]{3,2,1,0:T(8,128)(2,1)} %bitcast.234), kind=kLoop, calls=%fused_computation.85 | loop fusion | flops 2097152 | bytes 8388672 | tf_op jit(solution)/shard_map/jit(_where)/select_n | solution.py:166
  245.7 9.9 %all-to-all-start.2 = ((bf16[32,2,128,256]{3,1,2,0:T(2,128)(2,1)}), bf16[32,2,128,256]{3,1,2,0:T(2,128)(2,1)}, u32[]{:S(2)}, u32[]{:S(2)}) async-start(bf16[32,2,128,256]{3,1,2,0:T(2,128)(2,1)} %broadcast_select_fusion), calls=%async_computation.2 | async-start | bytes 8388608 | tf_op jit(solution)/shard_map/all_to_all | solution.py:167
  256.9 21.8 %psum.14 = f32[10]{0:T(128)S(1)} all-reduce(f32[10]{0:T(128)S(1)} %reshape.704), channel_id=1, replica_groups=mesh['dp'=16,'ctx'=32] {'dp'}, use_global_device_ids=true, to_apply=%region_12.13 | all-reduce | flops 10 | bytes 80 | tf_op jit(solution)/shard_map/psum | solution.py:194
  278.9 130.1 %psum.15 = f32[10]{0:T(128)} all-reduce(f32[10]{0:T(128)S(1)} %psum.14), channel_id=1, replica_groups=mesh['dp'=16,'ctx'=32] {'ctx'}, use_global_device_ids=true, to_apply=%region_13.14 | all-reduce | flops 10 | bytes 80 | tf_op jit(solution)/shard_map/psum | solution.py:194
  409.0 2.2 copy.170
  411.2 8.9 %copy.168 = bf16[32,2,128,256]{3,1,0,2:T(2,128)(2,1)} copy(bf16[32,2,128,256]{3,1,2,0:T(2,128)(2,1)} %all-to-all-done.2) | data formatting | bytes 8388608 | tf_op jit(solution)/shard_map/all_to_all | solution.py:167
  420.0 7.2 %reshape.728 = bf16[64,128,256,1]{2,0,1,3:T(8,128)(2,1)} reshape(bf16[32,2,128,256]{3,1,0,2:T(2,128)(2,1)} %copy.168) | data formatting | bytes 8388608 | tf_op jit(solution)/shard_map/reshape | solution.py:181
  427.3 4.9 %fusion.56 = f32[10,2,128,256]{3,0,2,1:T(8,128)} fusion(bf16[64,128,256,1]{2,0,1,3:T(8,128)(2,1)} %reshape.728, s32[10,2]{0,1:T(2,128)S(1)} %multiply_add_fusion, s32[64]{0:T(128)S(1)} %eq.67), kind=kOutput, calls=%fused_computation.97 | convolution fusion | flops 83887360 | bytes 6816080 | tf_op jit(solution)/shard_map/pj,pbe->jbe/dot_general | solution.py:178
  432.2 3.4 copy.169
  435.6 2.2 fusion.53
  437.9 1.1 copy.172
  438.9 1.1 copy.171
  (163 shorter events, 55.6 us)
Async XLA Ops:
  0.6 0.7 copy-start
  0.6 13.5 %copy-start.3 = (bf16[1,256,1280]{2,1,0:T(8,128)(2,1)S(1)}, bf16[1,256,1280]{2,1,0:T(8,128)(2,1)}, u32[]{:S(2)}) copy-start(bf16[1,256,1280]{2,1,0:T(8,128)(2,1)} %param.12) | copy-start | bytes 1966084
  2.7 13.6 %all-to-all-start = ((s32[32,1,2]{2,1,0:T(1,128)}), s32[32,1,2]{2,1,0:T(1,128)S(1)}, u32[]{:S(2)}, u32[]{:S(2)}) async-start(s32[32,1,2]{2,1,0:T(1,128)} %bitcast.31), calls=%async_computation | async-start | bytes 32768 | tf_op jit(solution)/shard_map/all_to_all | solution.py:113
  19.4 11.0 %copy-start.2 = (bf16[1,256,1280]{2,1,0:T(8,128)(2,1)S(1)}, bf16[1,256,1280]{2,1,0:T(8,128)(2,1)}, u32[]{:S(2)}) copy-start(bf16[1,256,1280]{2,1,0:T(8,128)(2,1)} %param.11) | copy-start | bytes 1966084
  19.4 101.2 %all-to-all-start.1 = ((bf16[32,2,128,256]{3,2,1,0:T(8,128)(2,1)}), bf16[32,2,128,256]{3,2,1,0:T(8,128)(2,1)}, u32[]{:S(2)}, u32[]{:S(2)}) async-start(bf16[32,2,128,256]{3,2,1,0:T(8,128)(2,1)} %bitcast.232), calls=%async_computation.1 | async-start | bytes 8388608 | tf_op jit(solution)/shard_map/all_to_all | solution.py:148
  30.1 0.8 copy-start.5
  30.1 1.1 copy-start.4
  245.7 165.4 %all-to-all-start.2 = ((bf16[32,2,128,256]{3,1,2,0:T(2,128)(2,1)}), bf16[32,2,128,256]{3,1,2,0:T(2,128)(2,1)}, u32[]{:S(2)}, u32[]{:S(2)}) async-start(bf16[32,2,128,256]{3,1,2,0:T(2,128)(2,1)} %broadcast_select_fusion), calls=%async_computation.2 | async-start | bytes 8388608 | tf_op jit(solution)/shard_map/all_to_all | solution.py:167
  435.6 4.5 %copy-start.1 = (s32[10,1,6]{0,1,2:T(1,128)S(1)}, s32[10,1,6]{0,1,2:T(1,128)}, u32[]{:S(2)}) copy-start(s32[10,1,6]{0,1,2:T(1,128)} %param.14) | copy-start | bytes 724
